TPU v7x, 32 devices: a whole 2x2x4 slice. The times are simulated.
32 devices in a mesh: region: 16 (over z, y, x), mp: 2 (over core).
Axes of the slice: x: 2, y: 2, z: 4, core: 2. Of those that a mesh axis runs over, the one named last changes fastest.
Arguments:
- tokens: bfloat16 [16384, 1024], P('region')
- ln_gain: bfloat16 [1024], replicated, may hold values from 0.25 to 1.75
- w_qkv: bfloat16 [1024, 3, 1024], P(None, None, 'mp')
- w_out: bfloat16 [1024, 1024], P('mp'), may hold values from -0.75 to 0.75
- neighbours: int32 [256, 8], P('region'), may hold values from 0 to 255, as said below
- degree: int32 [256], P('region'), may hold values from 1 to 8
Outputs:
- update: bfloat16 [16384, 1024], P('region')
Inputs may be any that keep to these rules, and one draw needn't show every extreme that they name: A neighbour of a patch with local index below 2 in its region (local index = id % 16, region = id // 16) lies in the same region or is one of the last 2 patches of region r-1 or r-2 (cyclically); of local index 14 or more: same region or one of the first 2 patches of region r+1 or r+2; any other patch's neighbours lie in its own region. Only the first degree[p] entries of a row count.
All inputs are finite; a program needn't handle non-finite values.
Results may differ from a plain program's by a relative error of at most 0.012.
The roundings to bfloat16 on the way count: a program that leaves them out, or rounds other values in their place, can miss the bound.
Values may be sent and summed in bfloat16 or wider, within the bound.
A program may use at most 192 MiB of HBM per device.

v0:
```python
import jax
import jax.numpy as jnp
from jax import lax
from jax.sharding import PartitionSpec as P

HDIM = 64
NBR = 8
RIM = 2


def spread_2(value, axis, source):
    kept = jnp.where(lax.axis_index(axis) == source, value, 0).astype(value.dtype)
    return lax.psum(kept, axis)


def from_behind(block, axis, distance):
    devices = range(lax.axis_size(axis))
    route = [((i - distance) % len(devices), i) for i in devices]
    return lax.ppermute(block, axis, route)


def layer_norm(rows, gain):
    values = rows.astype(jnp.float32)
    centre = jnp.mean(values, axis=-1, keepdims=True)
    spread = jnp.mean((values - centre) ** 2, axis=-1, keepdims=True)
    return ((values - centre) * lax.rsqrt(spread + 1e-05) * gain.astype(jnp.float32)).astype(
        jnp.bfloat16
    )


def project(block, w_flat, feat):
    out = jnp.dot(block, w_flat, preferred_element_type=jnp.float32).reshape(-1, 3, feat)
    query = (out[:, 0, :] * (1.0 / HDIM**0.5)).astype(jnp.bfloat16)
    pair = jnp.stack([out[:, 1, :].astype(jnp.bfloat16), out[:, 2, :].astype(jnp.bfloat16)], axis=1)
    return (query, pair)


def attend_block(query, pairs, valid, heads):
    npat, keys = (pairs.shape[0], pairs.shape[1])
    patch = query.shape[1]
    query = query.reshape(npat, patch, heads, HDIM)
    key_part = pairs[:, :, 0, :].reshape(npat, keys, heads, HDIM)
    value_part = pairs[:, :, 1, :].reshape(npat, keys, heads, HDIM)
    scores = jnp.einsum("pqhd,pkhd->phqk", query, key_part, preferred_element_type=jnp.float32)
    scores = jnp.where(valid[:, None, None, :], scores, jnp.float32(-1e30))
    top = jnp.max(scores, axis=-1, keepdims=True)
    expo = jnp.exp(scores - top)
    total = jnp.sum(expo, axis=-1)
    weights = expo.astype(jnp.bfloat16)
    context = jnp.einsum("phqk,pkhd->pqhd", weights, value_part, preferred_element_type=jnp.float32)
    context = context / jnp.transpose(total, (0, 2, 1))[..., None]
    return context.astype(jnp.bfloat16).reshape(npat * patch, heads * HDIM)


def per_device(tokens, ln_gain, w_qkv, w_out, neighbours, degree):
    rows, width = tokens.shape
    npat = neighbours.shape[0]
    patch = rows // npat
    feat = w_qkv.shape[2]
    heads_here = feat // HDIM
    rim = RIM
    normed = layer_norm(tokens, ln_gain)
    w_flat = w_qkv.reshape(width, 3 * feat)
    query, pairs = project(normed, w_flat, feat)
    kv_pat = pairs.reshape(npat, patch, 2, feat)
    anchor = spread_2(kv_pat[0], "region", 0)

    def fetch_before(step):
        return from_behind(kv_pat[npat - rim :], "region", step)

    def fetch_after(step):
        return from_behind(kv_pat[:rim], "region", step)

    table = jnp.concatenate(
        [kv_pat, fetch_before(1), fetch_before(2), fetch_after(-1), fetch_after(-2)], axis=0
    )
    cycle = lax.axis_size("region")
    region_id = lax.axis_index("region")
    owner = neighbours // npat
    local = neighbours % npat
    reach = (owner - region_id) % cycle
    slot = jnp.where(
        reach == 0,
        local,
        jnp.where(
            reach == cycle - 1,
            npat + local - (npat - rim),
            jnp.where(
                reach == cycle - 2,
                npat + rim + local - (npat - rim),
                jnp.where(reach == 1, npat + 2 * rim + local, npat + 3 * rim + local),
            ),
        ),
    )
    far = table[slot].reshape(npat, NBR * patch, 2, feat)
    anchors = jnp.broadcast_to(anchor[None], (npat, patch, 2, feat))
    keyed = jnp.concatenate([kv_pat, far, anchors], axis=1)
    slot_ok = jnp.arange(NBR, dtype=jnp.int32)[None, :] < degree[:, None]
    far_ok = jnp.repeat(slot_ok, patch, axis=1)
    ones = jnp.ones((npat, patch), dtype=bool)
    valid = jnp.concatenate([ones, far_ok, ones], axis=1)
    context = attend_block(query.reshape(npat, patch, feat), keyed, valid, heads_here)
    partial_sum = jnp.dot(context, w_out, preferred_element_type=jnp.float32)
    return lax.psum(partial_sum, "mp").astype(jnp.bfloat16)


def solution(mesh):
    placed = (
        P("region", None),
        P(),
        P(None, None, "mp"),
        P("mp", None),
        P("region", None),
        P("region"),
    )
    return jax.shard_map(
        per_device, mesh=mesh, in_specs=placed, out_specs=P("region", None), check_vma=False
    )
```

profile of v0, /device:TPU:0, one launch (start us, length us, event | category | flops | bytes accessed | tf_op | source)
XLA Modules:
  0.0 281.2 jit_solution(11935173775363583606)
XLA Ops:
  7.3 1.9 convert_reduce_fusion
  9.3 2.4 fusion.9
  11.7 4.7 %copy.11 = bf16[1024,3,512]{0,2,1:T(8,128)(2,1)} copy(bf16[1024,3,512]{2,0,1:T(8,128)(2,1)} %param.8) | data formatting | bytes 6291456 | tf_op args[2]
  16.4 7.5 %fusion.32 = (bf16[1024,3,512]{2,0,1:T(8,128)(2,1)S(1)}, f32[1024,3,512]{2,0,1:T(8,128)}) fusion(bf16[1024,3,512]{0,2,1:T(8,128)(2,1)} %copy.11, bf16[1024,1024]{1,0:T(8,128)(2,1)S(1)} %copy-done.3, f32[1024]{0:T(1024)S(1)} %convert_element_type.32, f32[1024]{0:T(1024)S(1)} %add_rsqrt_fusion, f32[1024]{0:T(1024)S(1)} %broadcast_multiply_fusion), kind=kOutput, calls=%fused_computation.57 | convolution fusion | flops 3228041216 | bytes 14692352 | tf_op jit(solution)/shard_map/dot_general | solution.py:32
  23.9 1.7 copy-done.4
  26.5 3.0 %collective-permute-start.1 = (bf16[2,64,2,512]{3,1,0,2:T(8,128)(2,1)}, bf16[2,64,2,512]{3,1,0,2:T(8,128)(2,1)}, u32[]{:S(2)}, u32[]{:S(2)}) collective-permute-start(bf16[2,64,2,512]{3,1,0,2:T(8,128)(2,1)} %bitcast.6), channel_id=1, source_target_pairs={{28,0},{30,2},{0,4},{2,6},{4,8},{6,10},{8,12},{10,14},{12,16},{14,... | collective-permute-start | bytes 786440 | tf_op jit(solution)/shard_map/ppermute | solution.py:19
  29.5 1.5 collective-permute-start
  30.9 3.2 %collective-permute-start.3 = (bf16[2,64,2,512]{3,1,0,2:T(8,128)(2,1)}, bf16[2,64,2,512]{3,1,0,2:T(8,128)(2,1)S(1)}, u32[]{:S(2)}, u32[]{:S(2)}) collective-permute-start(bf16[2,64,2,512]{3,1,0,2:T(8,128)(2,1)} %bitcast.7), channel_id=1, source_target_pairs={{4,0},{6,2},{8,4},{10,6},{12,8},{14,10},{16,12},{18,14},{20,16},{2... | collective-permute-start | bytes 786440 | tf_op jit(solution)/shard_map/ppermute | solution.py:19
  34.1 1.3 collective-permute-start.2
  35.4 1.6 slice_select_fusion
  37.0 1.7 fusion.31
  38.9 3.5 %fusion.19 = bf16[1024,1,512]{2,0,1:T(8,128)(2,1)} fusion(f32[1024,3,512]{2,0,1:T(8,128)} %get-tuple-element.12), kind=kLoop, calls=%fused_computation.23 | loop fusion | flops 1048576 | bytes 3145728 | tf_op jit(solution)/shard_map/convert_element_type | solution.py:33
  42.3 1.5 maximum_dynamic-update-slice_fusion
  44.3 3.0 %convert_element_type.35 = bf16[16,64,8,64]{3,2,1,0:T(8,128)(2,1)S(1)} reshape(bf16[1024,1,512]{2,0,1:T(8,128)(2,1)} %fusion.19) | data formatting | bytes 2097152 | tf_op jit(solution)/shard_map/convert_element_type | solution.py:33
  47.3 1.7 constant_dynamic-update-slice_fusion.3
  49.0 1.7 constant_dynamic-update-slice_fusion.2
  50.7 1.7 constant_dynamic-update-slice_fusion.1
  53.1 10.2 %gather_fusion = bf16[128,64,2,512]{3,1,2,0:T(8,128)(2,1)} fusion(bf16[24,64,2,512]{3,1,0,2:T(8,128)(2,1)} %constant_dynamic-update-slice_fusion, s32[1024]{0:T(1024)S(1)} %pad_clamp_fusion), kind=kCustom, calls=%fused_computation | custom fusion | bytes 33554944 | tf_op jit(solution)/shard_map/gather | solution.py:95
  63.3 14.1 %copy.13 = bf16[128,64,2,512]{3,1,0,2:T(8,128)(2,1)} copy(bf16[128,64,2,512]{3,1,2,0:T(8,128)(2,1)} %gather_fusion) | data formatting | bytes 33554432 | tf_op jit(solution)/shard_map/gather | solution.py:95
  77.4 65.8 %all-reduce.3.cloned.1.call-done = bf16[64,2,512]{2,0,1:T(8,128)(2,1)} async-done(((bf16[64,2,512]{2,0,1:T(8,128)(2,1)}), bf16[64,2,512]{2,0,1:T(8,128)(2,1)}) %all-reduce.3.cloned.1.call-update) | async-done | bytes 131088 | tf_op jit(solution)/shard_map/psum | solution.py:13
  143.1 2.5 broadcast_in_dim.41
  145.6 21.4 %pad_maximum_fusion = bf16[16,640,2,512]{3,1,0,2:T(8,128)(2,1)} fusion(bf16[16,64,2,512]{3,1,0,2:T(8,128)(2,1)} %broadcast_in_dim.41, bf16[16,512,2,512]{3,1,0,2:T(8,128)(2,1)} %bitcast.35, bf16[16,64,1,512]{3,1,0,2:T(8,128)(2,1)} %bitcast.40, bf16[16,64,1,512]{3,1,0,2:T(8,128)(2,1)} %bitcast.38), kind=kLoop, calls=%fused_computation.1 | loop fusion | flops 83886080 | bytes 41943040 | tf_op jit(solution)/shard_map/concatenate | solution.py:97
  167.0 16.1 %fusion.29 = (bf16[16,640,1,512]{3,1,0,2:T(8,128)(2,1)}, bf16[16,640,1,512]{3,1,0,2:T(8,128)(2,1)}) fusion(bf16[16,640,2,512]{3,1,0,2:T(8,128)(2,1)} %pad_maximum_fusion), kind=kLoop, calls=%fused_computation.54 | loop fusion | bytes 41943040 | tf_op jit(solution)/shard_map/slice | solution.py:42
  183.1 15.0 %copy.15 = bf16[16,640,1,512]{1,3,0,2:T(8,128)(2,1)} copy(bf16[16,640,1,512]{3,1,0,2:T(8,128)(2,1)} %get-tuple-element.5) | data formatting | bytes 20971520 | tf_op jit(solution)/shard_map/slice | solution.py:42
  198.1 14.5 %copy.14 = bf16[16,640,1,512]{1,3,0,2:T(8,128)(2,1)} copy(bf16[16,640,1,512]{3,1,0,2:T(8,128)(2,1)} %get-tuple-element.6) | data formatting | bytes 20971520 | tf_op jit(solution)/shard_map/slice | solution.py:43
  212.7 13.9 %select_reduce_fusion = (f32[16,8,64]{2,1,0:T(8,128)S(1)}, f32[16,8,64,640]{3,2,1,0:T(8,128)}) fusion(pred[16,640]{1,0:T(8,128)(4,1)S(1)} %pad_add_fusion, bf16[16,640,8,64]{1,3,2,0:T(8,128)(2,1)} %bitcast.34, bf16[16,64,8,64]{3,2,1,0:T(8,128)(2,1)S(1)} %convert_element_type.35), kind=kOutput, calls=%fused_computation.3 | convolution fusion | flops 681566208 | bytes 32548864 | tf_op jit(solution)/shard_map/pqhd,pkhd->phqk/dot_general | solution.py:44
  226.5 9.4 %fusion = f32[16,8,64]{2,1,0:T(8,128)S(1)} fusion(f32[16,8,64,640]{3,2,1,0:T(8,128)} %get-tuple-element.14, f32[16,8,64]{2,1,0:T(8,128)S(1)} %get-tuple-element.13, pred[16,640]{1,0:T(8,128)(4,1)S(1)} %pad_add_fusion), kind=kLoop, calls=%fused_computation.4 | loop fusion | flops 15720448 | bytes 21047296 | tf_op jit(solution)/shard_map/reduce_sum | solution.py:48
  236.0 13.5 %fusion.12 = bf16[16,64,8,64]{1,3,2,0:T(8,128)(2,1)} fusion(bf16[16,640,8,64]{1,3,2,0:T(8,128)(2,1)} %bitcast.36, f32[16,8,64,640]{3,2,1,0:T(8,128)} %get-tuple-element.14, f32[16,8,64]{2,1,0:T(8,128)S(1)} %get-tuple-element.13, pred[16,640]{1,0:T(8,128)(4,1)S(1)} %pad_add_fusion, f32[16,64,8]{1,2,0:T(8,128)S(1)} %bitcast.41), kind=kOutput, calls=%fused_computation.18 | convolution fusion | flops 687865856 | bytes 32581632 | tf_op jit(solution)/shard_map/phqk,pkhd->pqhd/dot_general | solution.py:50
  249.5 3.2 %copy.17 = bf16[16,64,8,64]{3,2,1,0:T(8,128)(2,1)S(1)} copy(bf16[16,64,8,64]{1,3,2,0:T(8,128)(2,1)} %fusion.12) | data formatting | bytes 2097152 | tf_op jit(solution)/shard_map/convert_element_type | solution.py:52
  252.8 2.0 reshape.46
  254.8 4.4 %fusion.33 = f32[1024,1024]{1,0:T(8,128)} fusion(bf16[1024,512]{1,0:T(8,128)(2,1)} %reshape.46, bf16[512,1024]{1,0:T(8,128)(2,1)S(1)} %copy-done), kind=kOutput, calls=%fused_computation.58 | convolution fusion | flops 1073741824 | bytes 6291456 | tf_op jit(solution)/shard_map/dot_general | solution.py:103
  259.2 15.1 %all-reduce.4 = bf16[1024,1024]{1,0:T(8,128)(2,1)} all-reduce(f32[1024,1024]{1,0:T(8,128)} %fusion.33), channel_id=1, replica_groups=mesh['region'=16,'mp'=2] {'mp'}, use_global_device_ids=true, to_apply=%region_5.6 | all-reduce | flops 1048576 | bytes 6291456 | tf_op jit(solution)/shard_map/psum | solution.py:104
  (33 shorter events, 2.9 us)
Async XLA Ops:
  6.5 248.3 %copy-start = (bf16[512,1024]{1,0:T(8,128)(2,1)S(1)}, bf16[512,1024]{1,0:T(8,128)(2,1)}, u32[]{:S(2)}) copy-start(bf16[512,1024]{1,0:T(8,128)(2,1)} %param.9) | copy-start | bytes 3145732
  6.5 136.6 %all-reduce.3.cloned.1.call-start = ((), (), s32[]{:S(2)}) async-start(), calls=%async_computation | async-start | bytes 262144 | tf_op jit(solution)/shard_map/psum | solution.py:13
  9.3 7.1 %copy-start.3 = (bf16[1024,1024]{1,0:T(8,128)(2,1)S(1)}, bf16[1024,1024]{1,0:T(8,128)(2,1)}, u32[]{:S(2)}) copy-start(bf16[1024,1024]{1,0:T(8,128)(2,1)} %param.6) | copy-start | bytes 6291460
  23.9 1.7 copy-start.4
  23.9 14.8 %copy-start.6 = (s32[16]{0:T(128)S(1)}, s32[16]{0:T(128)}, u32[]{:S(2)}) copy-start(s32[16]{0:T(128)} %param.11) | copy-start | bytes 196
  23.9 14.9 %copy-start.5 = (s32[16,8]{0,1:T(8,128)S(1)}, s32[16,8]{0,1:T(8,128)}, u32[]{:S(2)}) copy-start(s32[16,8]{0,1:T(8,128)} %param.10) | copy-start | bytes 1540
  26.5 22.5 %collective-permute-start.1 = (bf16[2,64,2,512]{3,1,0,2:T(8,128)(2,1)}, bf16[2,64,2,512]{3,1,0,2:T(8,128)(2,1)}, u32[]{:S(2)}, u32[]{:S(2)}) collective-permute-start(bf16[2,64,2,512]{3,1,0,2:T(8,128)(2,1)} %bitcast.6), channel_id=1, source_target_pairs={{28,0},{30,2},{0,4},{2,6},{4,8},{6,10},{8,12},{10,14},{12,16},{14,... | collective-permute-start | bytes 786440 | tf_op jit(solution)/shard_map/ppermute | solution.py:19
  29.5 17.8 %collective-permute-start = (bf16[2,64,2,512]{3,1,0,2:T(8,128)(2,1)}, bf16[2,64,2,512]{3,1,0,2:T(8,128)(2,1)}, u32[]{:S(2)}, u32[]{:S(2)}) collective-permute-start(bf16[2,64,2,512]{3,1,0,2:T(8,128)(2,1)} %bitcast.6), channel_id=1, source_target_pairs={{30,0},{0,2},{2,4},{4,6},{6,8},{8,10},{10,12},{12,14},{14,16},{16,... | collective-permute-start | bytes 786440 | tf_op jit(solution)/shard_map/ppermute | solution.py:19
  30.9 21.4 %collective-permute-start.3 = (bf16[2,64,2,512]{3,1,0,2:T(8,128)(2,1)}, bf16[2,64,2,512]{3,1,0,2:T(8,128)(2,1)S(1)}, u32[]{:S(2)}, u32[]{:S(2)}) collective-permute-start(bf16[2,64,2,512]{3,1,0,2:T(8,128)(2,1)} %bitcast.7), channel_id=1, source_target_pairs={{4,0},{6,2},{8,4},{10,6},{12,8},{14,10},{16,12},{18,14},{20,16},{2... | collective-permute-start | bytes 786440 | tf_op jit(solution)/shard_map/ppermute | solution.py:19
  34.1 16.5 %collective-permute-start.2 = (bf16[2,64,2,512]{3,1,0,2:T(8,128)(2,1)}, bf16[2,64,2,512]{3,1,0,2:T(8,128)(2,1)}, u32[]{:S(2)}, u32[]{:S(2)}) collective-permute-start(bf16[2,64,2,512]{3,1,0,2:T(8,128)(2,1)} %bitcast.7), channel_id=1, source_target_pairs={{2,0},{4,2},{6,4},{8,6},{10,8},{12,10},{14,12},{16,14},{18,16},{20... | collective-permute-start | bytes 786440 | tf_op jit(solution)/shard_map/ppermute | solution.py:19
  38.7 3.6 %copy-start.1 = (bf16[1024,1,512]{2,0,1:T(8,128)(2,1)}, bf16[1024,1,512]{2,0,1:T(8,128)(2,1)S(1)}, u32[]{:S(2)}) copy-start(bf16[1024,1,512]{2,0,1:T(8,128)(2,1)S(1)} %get-tuple-element.9) | copy-start | bytes 3145732
  38.7 5.1 %copy-start.2 = (bf16[1024,1,512]{2,0,1:T(8,128)(2,1)}, bf16[1024,1,512]{2,0,1:T(8,128)(2,1)S(1)}, u32[]{:S(2)}) copy-start(bf16[1024,1,512]{2,0,1:T(8,128)(2,1)S(1)} %get-tuple-element.10) | copy-start | bytes 3145732
Sparse Core Ops, SparseCore 0:
  37.2 105.9 all-reduce.2
where the time goes:
time: 283 us; the launch traced here: 281 us
  local copies, waits for them, and re-layouts  95.8 us (34%)
  waiting for transfers between devices  65.8 us (23%)
  other arithmetic  42.7 us (15%)
  matrix products  39.3 us (14%)
  blocking collectives  15.1 us (5%)
  between operations  13.5 us (5%)
  starting transfers between devices  8.96 us (3%)
    psum x1, waiting for transfers between devices, spread_2(): return lax.psum(kept, axis)  65.8 us
    slice x2, local copies, waits for them, and re-layouts, attend_block(): key_part = pairs[:, :, 0, :].reshape(npat, keys, heads, HDIM)  31.2 us
    gather x2, local copies, waits for them, and re-layouts, per_device(): far = table[slot].reshape(npat, NBR * patch, 2, feat)  24.3 us
    concatenate x1, other arithmetic, per_device(): keyed = jnp.concatenate([kv_pat, far, anchors], axis=1)  21.4 us
    psum x1, blocking collectives, per_device(): return lax.psum(partial_sum, 'mp').astype(jnp.bfloat16)  15.1 us
    slice x1, local copies, waits for them, and re-layouts, attend_block(): value_part = pairs[:, :, 1, :].reshape(npat, keys, heads, HDIM)  14.5 us
    dot_general x1, matrix products, attend_block(): jnp.einsum('pqhd,pkhd->phqk', query, key_part, preferred_element_type=jnp...  13.9 us
    dot_general x1, matrix products, attend_block(): jnp.einsum('phqk,pkhd->pqhd', weights, value_part, preferred_element_type...  13.5 us
  transfers between devices with their start and end apart: 5, of which 1 were waited for; matrix products, arithmetic and copies ran while one was open for 15% of the time, Pallas kernels for 0%

commit v1 on v0

--- a/solution.py
+++ b/solution.py
@@ -101,7 +101,7 @@
     valid = jnp.concatenate([ones, far_ok, ones], axis=1)
     context = attend_block(query.reshape(npat, patch, feat), keyed, valid, heads_here)
     partial_sum = jnp.dot(context, w_out, preferred_element_type=jnp.float32)
-    return lax.psum(partial_sum, "mp").astype(jnp.bfloat16)
+    return jnp.sum(lax.all_gather(partial_sum, "mp"), axis=0).astype(jnp.bfloat16)
 
 
 def solution(mesh):

time: 283 us -> 293 us (1.035)
  waiting for transfers between devices: 65.8 us -> 84.8 us
  blocking collectives: 15.1 us -> 0 us
  other arithmetic: 42.7 us -> 48.9 us
    all_gather x0 -> x1, waiting for transfers between devices: none -> 19.1 us  [per_device(): lax.all_gather(partial_sum, 'mp')]
    psum x1 -> x0, blocking collectives: 15.1 us -> none  [per_device(): return lax.psum(partial_sum, 'mp').astype(jnp.bfloat16)]
    reduce_sum x0 -> x1, other arithmetic: none -> 6.23 us  [per_device(): jnp.sum(lax.all_gather(partial_sum, 'mp'), axis=0).astype(jnp.bfloat16)]
  transfers between devices with their start and end apart: 5 -> 6, of which waited for: 1 -> 2; matrix products, arithmetic and copies ran while one was open for 15% -> 14% of each run, Pallas kernels for 0% -> 0%
where the time goes in v1:
time: 293 us; the launch traced here: 292 us
  local copies, waits for them, and re-layouts  96.1 us (33%)
  waiting for transfers between devices  84.8 us (29%)
  other arithmetic  48.9 us (17%)
  matrix products  39.4 us (13%)
  between operations  13.5 us (5%)
  starting transfers between devices  9.01 us (3%)
    psum x1, waiting for transfers between devices, spread_2(): return lax.psum(kept, axis)  65.7 us
    slice x2, local copies, waits for them, and re-layouts, attend_block(): key_part = pairs[:, :, 0, :].reshape(npat, keys, heads, HDIM)  30.9 us
    gather x2, local copies, waits for them, and re-layouts, per_device(): far = table[slot].reshape(npat, NBR * patch, 2, feat)  24.3 us
    concatenate x1, other arithmetic, per_device(): keyed = jnp.concatenate([kv_pat, far, anchors], axis=1)  21.3 us
    all_gather x1, waiting for transfers between devices, per_device(): lax.all_gather(partial_sum, 'mp')  19.1 us
    slice x1, local copies, waits for them, and re-layouts, attend_block(): value_part = pairs[:, :, 1, :].reshape(npat, keys, heads, HDIM)  15.1 us
    dot_general x1, matrix products, attend_block(): jnp.einsum('pqhd,pkhd->phqk', query, key_part, preferred_element_type=jnp...  13.9 us
    dot_general x1, matrix products, attend_block(): jnp.einsum('phqk,pkhd->pqhd', weights, value_part, preferred_element_type...  13.5 us
  transfers between devices with their start and end apart: 6, of which 2 were waited for; matrix products, arithmetic and copies ran while one was open for 14% of the time, Pallas kernels for 0%

profile of v1, /device:TPU:0, one launch (start us, length us, event | category | flops | bytes accessed | tf_op | source)
XLA Modules:
  0.0 291.6 jit_solution(17529020316450398031)
XLA Ops:
  7.3 1.9 convert_reduce_fusion
  9.3 2.4 fusion.9
  11.7 4.7 %copy.11 = bf16[1024,3,512]{0,2,1:T(8,128)(2,1)} copy(bf16[1024,3,512]{2,0,1:T(8,128)(2,1)} %param.8) | data formatting | bytes 6291456 | tf_op args[2]
  16.4 7.6 %fusion.32 = (bf16[1024,3,512]{2,0,1:T(8,128)(2,1)S(1)}, f32[1024,3,512]{2,0,1:T(8,128)}) fusion(bf16[1024,3,512]{0,2,1:T(8,128)(2,1)} %copy.11, bf16[1024,1024]{1,0:T(8,128)(2,1)S(1)} %copy-done.3, f32[1024]{0:T(1024)S(1)} %convert_element_type.32, f32[1024]{0:T(1024)S(1)} %add_rsqrt_fusion, f32[1024]{0:T(1024)S(1)} %broadcast_multiply_fusion), kind=kOutput, calls=%fused_computation.57 | convolution fusion | flops 3228041216 | bytes 14692352 | tf_op jit(solution)/shard_map/dot_general | solution.py:32
  24.0 1.7 copy-done.4
  26.5 3.0 %collective-permute-start.1 = (bf16[2,64,2,512]{3,1,0,2:T(8,128)(2,1)}, bf16[2,64,2,512]{3,1,0,2:T(8,128)(2,1)}, u32[]{:S(2)}, u32[]{:S(2)}) collective-permute-start(bf16[2,64,2,512]{3,1,0,2:T(8,128)(2,1)} %bitcast.6), channel_id=1, source_target_pairs={{28,0},{30,2},{0,4},{2,6},{4,8},{6,10},{8,12},{10,14},{12,16},{14,... | collective-permute-start | bytes 786440 | tf_op jit(solution)/shard_map/ppermute | solution.py:19
  29.5 1.5 collective-permute-start
  31.0 3.2 %collective-permute-start.3 = (bf16[2,64,2,512]{3,1,0,2:T(8,128)(2,1)}, bf16[2,64,2,512]{3,1,0,2:T(8,128)(2,1)S(1)}, u32[]{:S(2)}, u32[]{:S(2)}) collective-permute-start(bf16[2,64,2,512]{3,1,0,2:T(8,128)(2,1)} %bitcast.7), channel_id=1, source_target_pairs={{4,0},{6,2},{8,4},{10,6},{12,8},{14,10},{16,12},{18,14},{20,16},{2... | collective-permute-start | bytes 786440 | tf_op jit(solution)/shard_map/ppermute | solution.py:19
  35.5 1.6 slice_select_fusion
  37.1 1.7 fusion.31
  38.9 3.5 %fusion.19 = bf16[1024,1,512]{2,0,1:T(8,128)(2,1)} fusion(f32[1024,3,512]{2,0,1:T(8,128)} %get-tuple-element.12), kind=kLoop, calls=%fused_computation.23 | loop fusion | flops 1048576 | bytes 3145728 | tf_op jit(solution)/shard_map/convert_element_type | solution.py:33
  42.4 1.5 maximum_dynamic-update-slice_fusion
  44.4 3.0 %convert_element_type.35 = bf16[16,64,8,64]{3,2,1,0:T(8,128)(2,1)S(1)} reshape(bf16[1024,1,512]{2,0,1:T(8,128)(2,1)} %fusion.19) | data formatting | bytes 2097152 | tf_op jit(solution)/shard_map/convert_element_type | solution.py:33
  47.4 1.7 constant_dynamic-update-slice_fusion.3
  49.1 1.7 constant_dynamic-update-slice_fusion.2
  50.8 1.7 constant_dynamic-update-slice_fusion.1
  53.2 10.2 %gather_fusion = bf16[128,64,2,512]{3,1,2,0:T(8,128)(2,1)} fusion(bf16[24,64,2,512]{3,1,0,2:T(8,128)(2,1)} %constant_dynamic-update-slice_fusion, s32[1024]{0:T(1024)S(1)} %pad_clamp_fusion), kind=kCustom, calls=%fused_computation | custom fusion | bytes 33554944 | tf_op jit(solution)/shard_map/gather | solution.py:95
  63.3 14.2 %copy.13 = bf16[128,64,2,512]{3,1,0,2:T(8,128)(2,1)} copy(bf16[128,64,2,512]{3,1,2,0:T(8,128)(2,1)} %gather_fusion) | data formatting | bytes 33554432 | tf_op jit(solution)/shard_map/gather | solution.py:95
  77.5 65.7 %all-reduce.2.cloned.1.call-done = bf16[64,2,512]{2,0,1:T(8,128)(2,1)} async-done(((bf16[64,2,512]{2,0,1:T(8,128)(2,1)}), bf16[64,2,512]{2,0,1:T(8,128)(2,1)}) %all-reduce.2.cloned.1.call-update) | async-done | bytes 131088 | tf_op jit(solution)/shard_map/psum | solution.py:13
  143.2 2.5 broadcast_in_dim.41
  145.6 21.3 %pad_maximum_fusion = bf16[16,640,2,512]{3,1,0,2:T(8,128)(2,1)} fusion(bf16[16,64,2,512]{3,1,0,2:T(8,128)(2,1)} %broadcast_in_dim.41, bf16[16,512,2,512]{3,1,0,2:T(8,128)(2,1)} %bitcast.36, bf16[16,64,1,512]{3,1,0,2:T(8,128)(2,1)} %bitcast.41, bf16[16,64,1,512]{3,1,0,2:T(8,128)(2,1)} %bitcast.39), kind=kLoop, calls=%fused_computation.1 | loop fusion | flops 83886080 | bytes 41943040 | tf_op jit(solution)/shard_map/concatenate | solution.py:97
  166.9 16.2 %fusion.29 = (bf16[16,640,1,512]{3,1,0,2:T(8,128)(2,1)}, bf16[16,640,1,512]{3,1,0,2:T(8,128)(2,1)}) fusion(bf16[16,640,2,512]{3,1,0,2:T(8,128)(2,1)} %pad_maximum_fusion), kind=kLoop, calls=%fused_computation.54 | loop fusion | bytes 41943040 | tf_op jit(solution)/shard_map/slice | solution.py:42
  183.1 14.7 %copy.15 = bf16[16,640,1,512]{1,3,0,2:T(8,128)(2,1)} copy(bf16[16,640,1,512]{3,1,0,2:T(8,128)(2,1)} %get-tuple-element.5) | data formatting | bytes 20971520 | tf_op jit(solution)/shard_map/slice | solution.py:42
  197.8 15.1 %copy.14 = bf16[16,640,1,512]{1,3,0,2:T(8,128)(2,1)} copy(bf16[16,640,1,512]{3,1,0,2:T(8,128)(2,1)} %get-tuple-element.6) | data formatting | bytes 20971520 | tf_op jit(solution)/shard_map/slice | solution.py:43
  212.9 13.9 %select_reduce_fusion = (f32[16,8,64]{2,1,0:T(8,128)S(1)}, f32[16,8,64,640]{3,2,1,0:T(8,128)}) fusion(pred[16,640]{1,0:T(8,128)(4,1)S(1)} %pad_add_fusion, bf16[16,640,8,64]{1,3,2,0:T(8,128)(2,1)} %bitcast.35, bf16[16,64,8,64]{3,2,1,0:T(8,128)(2,1)S(1)} %convert_element_type.35), kind=kOutput, calls=%fused_computation.3 | convolution fusion | flops 681566208 | bytes 32548864 | tf_op jit(solution)/shard_map/pqhd,pkhd->phqk/dot_general | solution.py:44
  226.8 9.4 %fusion = f32[16,8,64]{2,1,0:T(8,128)S(1)} fusion(f32[16,8,64,640]{3,2,1,0:T(8,128)} %get-tuple-element.14, f32[16,8,64]{2,1,0:T(8,128)S(1)} %get-tuple-element.13, pred[16,640]{1,0:T(8,128)(4,1)S(1)} %pad_add_fusion), kind=kLoop, calls=%fused_computation.4 | loop fusion | flops 15720448 | bytes 21047296 | tf_op jit(solution)/shard_map/reduce_sum | solution.py:48
  236.2 13.5 %fusion.12 = bf16[16,64,8,64]{1,3,2,0:T(8,128)(2,1)} fusion(bf16[16,640,8,64]{1,3,2,0:T(8,128)(2,1)} %bitcast.37, f32[16,8,64,640]{3,2,1,0:T(8,128)} %get-tuple-element.14, f32[16,8,64]{2,1,0:T(8,128)S(1)} %get-tuple-element.13, pred[16,640]{1,0:T(8,128)(4,1)S(1)} %pad_add_fusion, f32[16,64,8]{1,2,0:T(8,128)S(1)} %bitcast.43), kind=kOutput, calls=%fused_computation.18 | convolution fusion | flops 687865856 | bytes 32581632 | tf_op jit(solution)/shard_map/phqk,pkhd->pqhd/dot_general | solution.py:50
  249.8 3.2 %copy.17 = bf16[16,64,8,64]{3,2,1,0:T(8,128)(2,1)S(1)} copy(bf16[16,64,8,64]{1,3,2,0:T(8,128)(2,1)} %fusion.12) | data formatting | bytes 2097152 | tf_op jit(solution)/shard_map/convert_element_type | solution.py:52
  253.0 2.0 reshape.46
  255.1 4.4 %fusion.33 = f32[1024,1024]{1,0:T(8,128)} fusion(bf16[1024,512]{1,0:T(8,128)(2,1)} %reshape.46, bf16[512,1024]{1,0:T(8,128)(2,1)S(1)} %copy-done), kind=kOutput, calls=%fused_computation.58 | convolution fusion | flops 1073741824 | bytes 6291456 | tf_op jit(solution)/shard_map/dot_general | solution.py:103
  259.5 19.1 %all-gather.3.cloned.1.call-done = f32[2048,1024]{1,0:T(8,128)} async-done(((f32[1024,1024]{1,0:T(8,128)}), f32[2048,1024]{1,0:T(8,128)}) %all-gather.3.cloned.1.call-update) | async-done | bytes 8388624 | tf_op jit(solution)/shard_map/all_gather | solution.py:104
  278.6 6.2 %reduce_sum.39 = bf16[1024,1024]{1,0:T(8,128)(2,1)} reduce(f32[2,1024,1024]{2,1,0:T(8,128)} %bitcast.42, f32[]{:T(128)} %constant.55.clone.1), dimensions={0}, to_apply=%region_5.6 | reduce | flops 1048576 | bytes 10485764 | tf_op jit(solution)/shard_map/reduce_sum | solution.py:104
  (36 shorter events, 4.3 us)
Async XLA Ops:
  6.5 248.5 %copy-start = (bf16[512,1024]{1,0:T(8,128)(2,1)S(1)}, bf16[512,1024]{1,0:T(8,128)(2,1)}, u32[]{:S(2)}) copy-start(bf16[512,1024]{1,0:T(8,128)(2,1)} %param.9) | copy-start | bytes 3145732
  6.5 136.6 %all-reduce.2.cloned.1.call-start = ((), (), s32[]{:S(2)}) async-start(), calls=%async_computation | async-start | bytes 262144 | tf_op jit(solution)/shard_map/psum | solution.py:13
  9.3 7.2 %copy-start.3 = (bf16[1024,1024]{1,0:T(8,128)(2,1)S(1)}, bf16[1024,1024]{1,0:T(8,128)(2,1)}, u32[]{:S(2)}) copy-start(bf16[1024,1024]{1,0:T(8,128)(2,1)} %param.6) | copy-start | bytes 6291460
  24.0 1.7 copy-start.4
  24.0 14.8 %copy-start.6 = (s32[16]{0:T(128)S(1)}, s32[16]{0:T(128)}, u32[]{:S(2)}) copy-start(s32[16]{0:T(128)} %param.11) | copy-start | bytes 196
  24.0 14.9 %copy-start.5 = (s32[16,8]{0,1:T(8,128)S(1)}, s32[16,8]{0,1:T(8,128)}, u32[]{:S(2)}) copy-start(s32[16,8]{0,1:T(8,128)} %param.10) | copy-start | bytes 1540
  26.5 22.6 %collective-permute-start.1 = (bf16[2,64,2,512]{3,1,0,2:T(8,128)(2,1)}, bf16[2,64,2,512]{3,1,0,2:T(8,128)(2,1)}, u32[]{:S(2)}, u32[]{:S(2)}) collective-permute-start(bf16[2,64,2,512]{3,1,0,2:T(8,128)(2,1)} %bitcast.6), channel_id=1, source_target_pairs={{28,0},{30,2},{0,4},{2,6},{4,8},{6,10},{8,12},{10,14},{12,16},{14,... | collective-permute-start | bytes 786440 | tf_op jit(solution)/shard_map/ppermute | solution.py:19
  29.5 17.9 %collective-permute-start = (bf16[2,64,2,512]{3,1,0,2:T(8,128)(2,1)}, bf16[2,64,2,512]{3,1,0,2:T(8,128)(2,1)}, u32[]{:S(2)}, u32[]{:S(2)}) collective-permute-start(bf16[2,64,2,512]{3,1,0,2:T(8,128)(2,1)} %bitcast.6), channel_id=1, source_target_pairs={{30,0},{0,2},{2,4},{4,6},{6,8},{8,10},{10,12},{12,14},{14,16},{16,... | collective-permute-start | bytes 786440 | tf_op jit(solution)/shard_map/ppermute | solution.py:19
  31.0 21.5 %collective-permute-start.3 = (bf16[2,64,2,512]{3,1,0,2:T(8,128)(2,1)}, bf16[2,64,2,512]{3,1,0,2:T(8,128)(2,1)S(1)}, u32[]{:S(2)}, u32[]{:S(2)}) collective-permute-start(bf16[2,64,2,512]{3,1,0,2:T(8,128)(2,1)} %bitcast.7), channel_id=1, source_target_pairs={{4,0},{6,2},{8,4},{10,6},{12,8},{14,10},{16,12},{18,14},{20,16},{2... | collective-permute-start | bytes 786440 | tf_op jit(solution)/shard_map/ppermute | solution.py:19
  34.2 16.6 %collective-permute-start.2 = (bf16[2,64,2,512]{3,1,0,2:T(8,128)(2,1)}, bf16[2,64,2,512]{3,1,0,2:T(8,128)(2,1)}, u32[]{:S(2)}, u32[]{:S(2)}) collective-permute-start(bf16[2,64,2,512]{3,1,0,2:T(8,128)(2,1)} %bitcast.7), channel_id=1, source_target_pairs={{2,0},{4,2},{6,4},{8,6},{10,8},{12,10},{14,12},{16,14},{18,16},{20... | collective-permute-start | bytes 786440 | tf_op jit(solution)/shard_map/ppermute | solution.py:19
  37.1 241.5 %all-gather.3.cloned.1.call-start = ((), (), s32[]{:S(2)}) async-start(), calls=%async_computation.1 | async-start | bytes 12582912 | tf_op jit(solution)/shard_map/all_gather | solution.py:104
  38.8 3.6 %copy-start.1 = (bf16[1024,1,512]{2,0,1:T(8,128)(2,1)}, bf16[1024,1,512]{2,0,1:T(8,128)(2,1)S(1)}, u32[]{:S(2)}) copy-start(bf16[1024,1,512]{2,0,1:T(8,128)(2,1)S(1)} %get-tuple-element.9) | copy-start | bytes 3145732
  38.8 5.1 %copy-start.2 = (bf16[1024,1,512]{2,0,1:T(8,128)(2,1)}, bf16[1024,1,512]{2,0,1:T(8,128)(2,1)S(1)}, u32[]{:S(2)}) copy-start(bf16[1024,1,512]{2,0,1:T(8,128)(2,1)S(1)} %get-tuple-element.10) | copy-start | bytes 3145732
Sparse Core Ops, SparseCore 0:
  37.2 105.9 all-reduce.1
  259.6 18.8 all-gather.2
